TPU v7x, 256 devices: a whole 4x4x8 slice. The times are simulated.
256 devices in a mesh: blk: 32 (over z, x), span: 8 (over y, core).
Axes of the slice: x: 4, y: 4, z: 8, core: 2. Of those that a mesh axis runs over, the one named last changes fastest.
Arguments:
- fluid_adjoint_in: float32 [5, 256, 256, 128], P(None, 'blk', 'span'), may hold values from -4 to 4
- fluid_source: float32 [5, 256, 256, 128], P(None, 'blk', 'span'), may hold values from -24 to 24
- velocity: float32 [3, 256, 256, 128], P(None, 'blk', 'span'), may hold values from 0.1 to 1
- diffusion: float32 [5], replicated, may hold values from 0.5 to 2
- jacobian: float32 [5, 5], replicated, may hold values from -0.4 to 0.4
- wall_coefficient: float32 [32, 256, 128], P('blk', 'span'), may hold values from 0.5 to 2
- metal_costate_prior: float32 [512, 256, 128], P('blk', 'span'), may hold values from -4 to 4
- solid_source: float32 [512, 256, 128], P('blk', 'span'), may hold values from -12 to 12
- conductivity: float32 [512, 256, 128], P('blk', 'span'), may hold values from 0.3 to 3
- tile_owner: int32 [8, 1024, 1], P('span', 'blk'), may hold values from 0 to 31; in each aligned block of 32 rows (0 to 31, 32 to 63, ..., all dimensions but the last counted through in order) at most 3 rows name the same one
- tile_target: int32 [8, 1024], P('span', 'blk'), may hold values from 0 to 31
Outputs:
- fluid_adjoint: float32 [5, 256, 256, 128], P(None, 'blk', 'span')
- solid_adjoint: float32 [512, 256, 128], P('blk', 'span')
- residual_norms: float32 [6], replicated
Inputs may be any that keep to these rules, and one draw needn't show every extreme that they name: `tile_owner`: within the 32 wall tiles of one fluid block (the rows of one device), no owner is named more than 3 times, a bound that some block reaches; every owner is named by some tile.
All inputs are finite; a program needn't handle non-finite values.
Results may differ from a plain program's by a relative error of at most 0.004.
Values sent between devices are 32-bit elements; how exact they have to be, the bound alone decides.
A program may use at most 64 MiB of HBM per device.

v0:
```python
import jax
import jax.numpy as jnp
from jax import lax
from jax.sharding import PartitionSpec as P

FSWEEPS = 4
SSWEEPS = 4
damping_weight = 0.8


def padded(block, sides, width):
    for axis, dim in sides:
        count = lax.axis_size(axis)
        forward = [(i, i + 1) for i in range(count - 1)]
        backward = [(target, source) for source, target in forward]
        low = lax.ppermute(
            lax.slice_in_dim(block, block.shape[dim] - width, None, axis=dim), axis, forward
        )
        high = lax.ppermute(lax.slice_in_dim(block, 0, width, axis=dim), axis, backward)
        block = jnp.concatenate([low, block, high], axis=dim)
    return block


def fluid_operator(bordered_grid_data, velocity, spread, jacobian):
    centre = bordered_grid_data[:, 1:-1, 1:-1, 1:-1]
    x_next = bordered_grid_data[:, 2:, 1:-1, 1:-1]
    y_next = bordered_grid_data[:, 1:-1, 2:, 1:-1]
    z_next = bordered_grid_data[:, 1:-1, 1:-1, 2:]
    beside_all = (
        x_next
        + bordered_grid_data[:, :-2, 1:-1, 1:-1]
        + y_next
        + bordered_grid_data[:, 1:-1, :-2, 1:-1]
        + z_next
        + bordered_grid_data[:, 1:-1, 1:-1, :-2]
    )
    mixing = jnp.einsum("fg,gxyz->fxyz", jacobian, centre, precision=lax.Precision.HIGHEST)
    velocity_sum = velocity[0] + velocity[1] + velocity[2]
    return (
        (6.0 * spread + velocity_sum) * centre
        - spread * beside_all
        - velocity[0] * x_next
        - velocity[1] * y_next
        - velocity[2] * z_next
        + mixing
    )


def face_conductance(kappa_rim):
    centre = kappa_rim[1:-1, 1:-1, 1:-1]
    return (
        0.5 * (centre + kappa_rim[2:, 1:-1, 1:-1]),
        0.5 * (centre + kappa_rim[:-2, 1:-1, 1:-1]),
        0.5 * (centre + kappa_rim[1:-1, 2:, 1:-1]),
        0.5 * (centre + kappa_rim[1:-1, :-2, 1:-1]),
        0.5 * (centre + kappa_rim[1:-1, 1:-1, 2:]),
        0.5 * (centre + kappa_rim[1:-1, 1:-1, :-2]),
    )


def solid_operator(bordered_grid_data, faces, diagonal):
    centre = bordered_grid_data[1:-1, 1:-1, 1:-1]
    flows = (
        faces[0] * bordered_grid_data[2:, 1:-1, 1:-1]
        + faces[1] * bordered_grid_data[:-2, 1:-1, 1:-1]
    )
    flows = (
        flows
        + faces[2] * bordered_grid_data[1:-1, 2:, 1:-1]
        + faces[3] * bordered_grid_data[1:-1, :-2, 1:-1]
    )
    flows = (
        flows
        + faces[4] * bordered_grid_data[1:-1, 1:-1, 2:]
        + faces[5] * bordered_grid_data[1:-1, 1:-1, :-2]
    )
    return diagonal * centre - flows


def pad_depth(array):
    widths = [(0, 0)] * (array.ndim - 1) + [(1, 1)]
    return jnp.pad(array, widths)


def shards(
    fluid_adjoint_in,
    fluid_source,
    velocity,
    diffusion,
    jacobian,
    wall_coefficient,
    metal_costate_prior,
    solid_source,
    conductivity,
    tile_owner,
    tile_target,
):
    highest = lax.Precision.HIGHEST
    spread = diffusion[:, None, None, None]
    fluid_diagonal = (
        6.0 * spread
        + (velocity[0] + velocity[1] + velocity[2])
        + jnp.diagonal(jacobian)[:, None, None, None]
    )
    adjoint = fluid_adjoint_in
    for iteration in range(FSWEEPS):
        bordered_grid_data = padded(adjoint, (("blk", 1), ("span", 2)), 1)
        bordered_grid_data = pad_depth(bordered_grid_data)
        fluid_residual = fluid_source - fluid_operator(
            bordered_grid_data, velocity, spread, jacobian
        )
        adjoint = adjoint + damping_weight * fluid_residual / fluid_diagonal
    fluid_squares = jnp.sum(fluid_residual * fluid_residual, axis=(1, 2, 3))
    wall_flux = wall_coefficient[0] * adjoint[4, 0]
    rows = wall_flux.shape[0]
    blocks = lax.axis_size("blk")
    myself = lax.axis_index("blk")
    owner_local = tile_owner[0, :, 0]
    target_local = tile_target[0, :]
    owners_all, targets_all = (
        lax.all_gather(owner_local, "blk", axis=0, tiled=True),
        lax.all_gather(target_local, "blk", axis=0, tiled=True),
    )
    owner_grid = owners_all.reshape(blocks, rows)
    target_grid = targets_all.reshape(blocks, rows)
    to_myself = owner_grid == myself
    target_hot = target_grid[:, :, None] == jnp.arange(rows, dtype=jnp.int32)[None, None, :]
    placing = (target_hot & to_myself[:, :, None]).astype(jnp.float32).reshape(blocks * rows, rows)
    arrived = lax.all_gather(wall_flux, "blk", axis=0, tiled=True)
    surface = jnp.dot(placing.T, arrived, precision=highest)
    heat_source = solid_source.at[-1].add(surface)
    thermal_state_grid = metal_costate_prior
    kappa_rim = padded(conductivity, (("blk", 0), ("span", 1)), 1)
    kappa_rim = pad_depth(kappa_rim)
    faces = face_conductance(kappa_rim)
    metal_pivot_entries = faces[0] + faces[1] + faces[2] + faces[3] + faces[4] + faces[5]
    for iteration in range(SSWEEPS):
        bordered_grid_data = padded(thermal_state_grid, (("blk", 0), ("span", 1)), 1)
        bordered_grid_data = pad_depth(bordered_grid_data)
        metal_imbalance_grid = heat_source - solid_operator(
            bordered_grid_data, faces, metal_pivot_entries
        )
        thermal_state_grid = (
            thermal_state_grid + damping_weight * metal_imbalance_grid / metal_pivot_entries
        )
    interface_heat_level = thermal_state_grid[-1]
    boundary_patches_finished = lax.all_gather(interface_heat_level, "blk", axis=0, tiled=True)
    output_entries = jnp.take(boundary_patches_finished, owner_local * rows + target_local, axis=0)
    gas_outcome = adjoint.at[4, 0].add(wall_coefficient[0] * output_entries)
    solid_squares = jnp.sum(metal_imbalance_grid * metal_imbalance_grid)[None]
    totals = lax.psum(jnp.concatenate([fluid_squares, solid_squares]), ("blk", "span"))
    every_processor = lax.axis_size("blk") * lax.axis_size("span")
    fluid_cells = float(adjoint.shape[1] * adjoint.shape[2] * adjoint.shape[3] * every_processor)
    solid_cells = float(
        thermal_state_grid.shape[0]
        * thermal_state_grid.shape[1]
        * thermal_state_grid.shape[2]
        * every_processor
    )
    counts = jnp.array([fluid_cells] * 5 + [solid_cells], jnp.float32)
    magnitude_list = jnp.sqrt(totals / counts)
    return (gas_outcome, thermal_state_grid, magnitude_list)


def solution(mesh):
    placed = (
        P(None, "blk", "span", None),
        P(None, "blk", "span", None),
        P(None, "blk", "span", None),
        P(),
        P(),
        P("blk", "span", None),
        P("blk", "span", None),
        P("blk", "span", None),
        P("blk", "span", None),
        P("span", "blk", None),
        P("span", "blk"),
    )
    return jax.shard_map(
        shards,
        mesh=mesh,
        in_specs=placed,
        out_specs=(P(None, "blk", "span", None), P("blk", "span", None), P()),
        check_vma=False,
    )
```

profile of v0, /device:TPU:2, one launch (start us, length us, event | category | flops | bytes accessed | tf_op | source)
XLA Modules:
  0.0 370.5 jit_solution(5415000750408817278)
XLA Ops:
  0.7 1.6 copy.36
  3.0 3.4 collective-permute-start.1
  6.4 2.4 collective-permute-start
  9.6 3.4 collective-permute-start.17
  13.0 2.4 collective-permute-start.16
  15.5 3.4 collective-permute-start.21
  20.5 26.2 %all-reduce.11 = (s32[1024]{0:T(1024)S(1)}, s32[1024]{0:T(1024)S(1)}) all-reduce(s32[1024]{0:T(1024)S(1)} %bitcast_dynamic-update-slice_fusion.1, s32[1024]{0:T(1024)S(1)} %bitcast_dynamic-update-slice_fusion), channel_id=2, replica_groups=mesh['blk'=32,'span'=8] {'blk'}, use_global_device_ids=true, to_apply=%add.9 | all-reduce | flops 2048 | bytes 16384
  47.4 2.5 collective-permute-start.20
  50.5 1.3 collective-permute-start.2
  51.8 3.0 collective-permute-start.3
  56.2 3.7 %collective-permute-start.19 = (f32[18,1,128]{2,1,0:T(1,128)S(1)}, f32[18,1,128]{2,1,0:T(1,128)S(1)}, u32[]{:S(2)}, u32[]{:S(2)}) collective-permute-start(f32[18,1,128]{2,1,0:T(1,128)S(1)} %get-tuple-element.70), channel_id=1, source_target_pairs={{0,1},{1,2},{2,3},{3,4},{4,5},{5,6},{6,7},{8,9},{9,10},{10,11},{11... | collective-permute-start | bytes 27656 | tf_op jit(solution)/shard_map/ppermute | solution.py:16
  60.7 2.7 fusion.10
  63.4 1.9 collective-permute-start.4
  65.4 3.9 %collective-permute-start.5 = (f32[5,1,32,128]{3,0,2,1:T(8,128)S(1)}, f32[5,1,32,128]{3,0,2,1:T(8,128)S(1)}, u32[]{:S(2)}, u32[]{:S(2)}) collective-permute-start(f32[5,1,32,128]{3,0,2,1:T(8,128)S(1)} %get-tuple-element.56), channel_id=1, source_target_pairs={{0,8},{8,16},{16,24},{24,32},{32,40},{40,48},{48,56},{56,64},{64,7... | collective-permute-start | bytes 245768 | tf_op jit(solution)/shard_map/ppermute | solution.py:16
  69.3 1.7 collective-permute-done.4
  71.0 1.9 collective-permute-done.5
  72.9 1.3 collective-permute-start.6
  74.2 3.1 collective-permute-start.7
  79.0 2.2 fusion.11
  81.2 1.9 collective-permute-start.8
  83.1 4.2 %collective-permute-start.9 = (f32[5,1,32,128]{3,0,2,1:T(8,128)S(1)}, f32[5,1,32,128]{3,0,2,1:T(8,128)S(1)}, u32[]{:S(2)}, u32[]{:S(2)}) collective-permute-start(f32[5,1,32,128]{3,0,2,1:T(8,128)S(1)} %get-tuple-element.54), channel_id=1, source_target_pairs={{0,8},{8,16},{16,24},{24,32},{32,40},{40,48},{48,56},{56,64},{64,7... | collective-permute-start | bytes 245768 | tf_op jit(solution)/shard_map/ppermute | solution.py:16
  87.3 1.4 collective-permute-done.8
  88.7 1.8 collective-permute-done.9
  91.8 3.3 collective-permute-start.11
  96.5 5.7 %collective-permute-start.23 = (f32[18,1,128]{2,1,0:T(1,128)S(1)}, f32[18,1,128]{2,1,0:T(1,128)S(1)}, u32[]{:S(2)}, u32[]{:S(2)}) collective-permute-start(f32[18,1,128]{2,1,0:T(1,128)S(1)} %get-tuple-element.72), channel_id=1, source_target_pairs={{0,1},{1,2},{2,3},{3,4},{4,5},{5,6},{6,7},{8,9},{9,10},{10,11},{11... | collective-permute-start | bytes 27656 | tf_op jit(solution)/shard_map/ppermute | solution.py:16
  103.0 2.2 fusion.12
  105.2 1.9 collective-permute-start.12
  107.2 3.9 %collective-permute-start.13 = (f32[5,1,32,128]{3,0,2,1:T(8,128)S(1)}, f32[5,1,32,128]{3,0,2,1:T(8,128)S(1)}, u32[]{:S(2)}, u32[]{:S(2)}) collective-permute-start(f32[5,1,32,128]{3,0,2,1:T(8,128)S(1)} %get-tuple-element.52), channel_id=1, source_target_pairs={{0,8},{8,16},{16,24},{24,32},{32,40},{40,48},{48,56},{56,64},{64,7... | collective-permute-start | bytes 245768 | tf_op jit(solution)/shard_map/ppermute | solution.py:16
  112.4 2.3 collective-permute-done.13
  114.7 1.4 collective-permute-start.14
  116.2 3.1 collective-permute-start.15
  121.0 2.5 multiply_reduce_fusion
  123.5 59.1 %all_gather.14 = f32[1024,128]{1,0:T(8,128)S(1)} all-gather(f32[32,128]{1,0:T(8,128)S(1)} %bitcast_multiply_fusion), channel_id=1, replica_groups=mesh['blk'=32,'span'=8] {'blk'}, dimensions={0}, use_global_device_ids=true | all-gather | bytes 540672 | tf_op jit(solution)/shard_map/all_gather | solution.py:129
  184.0 1.9 collective-permute-start.24
  186.0 3.9 %collective-permute-start.25 = (f32[1,32,128]{2,1,0:T(8,128)S(1)}, f32[1,32,128]{2,1,0:T(8,128)S(1)}, u32[]{:S(2)}, u32[]{:S(2)}) collective-permute-start(f32[1,32,128]{2,1,0:T(8,128)S(1)} %get-tuple-element.78), channel_id=1, source_target_pairs={{0,8},{8,16},{16,24},{24,32},{32,40},{40,48},{48,56},{56,64},{64,7... | collective-permute-start | bytes 49160 | tf_op jit(solution)/shard_map/ppermute | solution.py:16
  189.9 1.7 collective-permute-done.25
  191.6 1.3 collective-permute-start.26
  192.9 3.0 collective-permute-start.27
  197.5 1.9 collective-permute-start.28
  199.4 3.9 %collective-permute-start.29 = (f32[1,32,128]{2,1,0:T(8,128)S(1)}, f32[1,32,128]{2,1,0:T(8,128)S(1)}, u32[]{:S(2)}, u32[]{:S(2)}) collective-permute-start(f32[1,32,128]{2,1,0:T(8,128)S(1)} %get-tuple-element.76), channel_id=1, source_target_pairs={{0,8},{8,16},{16,24},{24,32},{32,40},{40,48},{48,56},{56,64},{64,7... | collective-permute-start | bytes 49160 | tf_op jit(solution)/shard_map/ppermute | solution.py:16
  203.4 1.7 collective-permute-done.29
  206.4 5.1 %collective-permute-start.31 = (f32[18,1,128]{2,1,0:T(1,128)S(1)}, f32[18,1,128]{2,1,0:T(1,128)S(1)}, u32[]{:S(2)}, u32[]{:S(2)}) collective-permute-start(f32[18,1,128]{2,1,0:T(1,128)S(1)} %get-tuple-element.66), channel_id=1, source_target_pairs={{0,1},{1,2},{2,3},{3,4},{4,5},{5,6},{6,7},{8,9},{9,10},{10,11},{11... | collective-permute-start | bytes 27656 | tf_op jit(solution)/shard_map/ppermute | solution.py:16
  213.1 1.9 collective-permute-start.32
  215.0 4.2 %collective-permute-start.33 = (f32[1,32,128]{2,1,0:T(8,128)S(1)}, f32[1,32,128]{2,1,0:T(8,128)S(1)}, u32[]{:S(2)}, u32[]{:S(2)}) collective-permute-start(f32[1,32,128]{2,1,0:T(8,128)S(1)} %get-tuple-element.74), channel_id=1, source_target_pairs={{0,8},{8,16},{16,24},{24,32},{32,40},{40,48},{48,56},{56,64},{64,7... | collective-permute-start | bytes 49160 | tf_op jit(solution)/shard_map/ppermute | solution.py:16
  219.3 1.4 collective-permute-done.33
  222.0 4.8 %collective-permute-start.35 = (f32[18,1,128]{2,1,0:T(1,128)S(1)}, f32[18,1,128]{2,1,0:T(1,128)S(1)}, u32[]{:S(2)}, u32[]{:S(2)}) collective-permute-start(f32[18,1,128]{2,1,0:T(1,128)S(1)} %get-tuple-element.64), channel_id=1, source_target_pairs={{0,1},{1,2},{2,3},{3,4},{4,5},{5,6},{6,7},{8,9},{9,10},{10,11},{11... | collective-permute-start | bytes 27656 | tf_op jit(solution)/shard_map/ppermute | solution.py:16
  229.6 89.1 %psum.7 = f32[6]{0:T(128)S(1)} all-reduce(f32[6]{0:T(128)S(1)} %pad_maximum_fusion.78), channel_id=1, replica_groups=mesh['blk'=32,'span'=8] {'blk','span'}, use_global_device_ids=true, to_apply=%region_2.3 | all-reduce | flops 6 | bytes 48 | tf_op jit(solution)/shard_map/psum | solution.py:151
  318.9 49.3 %all-gather.2 = f32[1,1024,128]{2,1,0:T(8,128)S(1)} all-gather(f32[1,32,128]{2,1,0:T(8,128)S(1)} %slice.616), channel_id=4, replica_groups=mesh['blk'=32,'span'=8] {'blk'}, dimensions={1}, use_global_device_ids=true | all-gather | bytes 540672 | tf_op jit(solution)/shard_map/all_gather | solution.py:147
  (137 shorter events, 26.1 us)
Async XLA Ops:
  0.6 46.1 %copy-start = (f32[5,5]{1,0:T(8,128)S(1)}, f32[5,5]{1,0:T(8,128)}, u32[]{:S(2)}) copy-start(f32[5,5]{1,0:T(8,128)} %param.20) | copy-start | bytes 304
  0.6 18.4 %copy-start.18 = (u32[256]{0:T(256)S(1)}, u32[256]{0:T(256)}, u32[]{:S(2)}) copy-start(u32[256]{0:T(256)} %constant.146) | copy-start | bytes 3076
  0.7 49.3 %copy-start.3 = (f32[5,8,32,128]{3,2,1,0:T(8,128)S(1)}, f32[5,8,32,128]{3,2,1,0:T(8,128)}, u32[]{:S(2)}) copy-start(f32[5,8,32,128]{3,2,1,0:T(8,128)} %param.16) | copy-start | bytes 1966084
  0.7 49.2 %copy-start.1 = (f32[16,32,128]{2,1,0:T(8,128)S(1)}, f32[16,32,128]{2,1,0:T(8,128)}, u32[]{:S(2)}) copy-start(f32[16,32,128]{2,1,0:T(8,128)} %param.24) | copy-start | bytes 786436
  0.7 19.6 %copy-start.17 = (s32[1,32,1]{1,2,0:T(1,128)S(1)}, s32[1,32,1]{1,2,0:T(1,128)}, u32[]{:S(2)}) copy-start(s32[1,32,1]{1,2,0:T(1,128)} %param.25) | copy-start | bytes 388
  0.7 19.7 %copy-start.16 = (s32[1,32]{1,0:T(1,128)S(1)}, s32[1,32]{1,0:T(1,128)}, u32[]{:S(2)}) copy-start(s32[1,32]{1,0:T(1,128)} %param.26) | copy-start | bytes 388
  3.0 46.9 %collective-permute-start.1 = (f32[5,1,32,128]{3,0,2,1:T(8,128)}, f32[5,1,32,128]{3,0,2,1:T(8,128)S(1)}, u32[]{:S(2)}, u32[]{:S(2)}) collective-permute-start(f32[5,1,32,128]{3,0,2,1:T(8,128)} %get-tuple-element.59), channel_id=1, source_target_pairs={{0,8},{8,16},{16,24},{24,32},{32,40},{40,48},{48,56},{56,64},{64,7... | collective-permute-start | bytes 245768 | tf_op jit(solution)/shard_map/ppermute | solution.py:16
  6.4 44.0 %collective-permute-start = (f32[5,1,32,128]{3,0,2,1:T(8,128)}, f32[5,1,32,128]{3,0,2,1:T(8,128)S(1)}, u32[]{:S(2)}, u32[]{:S(2)}) collective-permute-start(f32[5,1,32,128]{3,0,2,1:T(8,128)} %get-tuple-element.58), channel_id=1, source_target_pairs={{8,0},{16,8},{24,16},{32,24},{40,32},{48,40},{56,48},{64,56},{72,6... | collective-permute-start | bytes 245768 | tf_op jit(solution)/shard_map/ppermute | solution.py:19
  9.6 37.7 %collective-permute-start.17 = (f32[1,32,128]{2,1,0:T(8,128)S(1)}, f32[1,32,128]{2,1,0:T(8,128)S(1)}, u32[]{:S(2)}, u32[]{:S(2)}) collective-permute-start(f32[1,32,128]{2,1,0:T(8,128)S(1)} %get-tuple-element.80), channel_id=1, source_target_pairs={{0,8},{8,16},{16,24},{24,32},{32,40},{40,48},{48,56},{56,64},{64,7... | collective-permute-start | bytes 49160 | tf_op jit(solution)/shard_map/ppermute | solution.py:16
  13.0 36.9 %collective-permute-start.16 = (f32[1,32,128]{2,1,0:T(8,128)S(1)}, f32[1,32,128]{2,1,0:T(8,128)S(1)}, u32[]{:S(2)}, u32[]{:S(2)}) collective-permute-start(f32[1,32,128]{2,1,0:T(8,128)S(1)} %get-tuple-element.81), channel_id=1, source_target_pairs={{8,0},{16,8},{24,16},{32,24},{40,32},{48,40},{56,48},{64,56},{72,6... | collective-permute-start | bytes 49160 | tf_op jit(solution)/shard_map/ppermute | solution.py:19
  15.5 49.9 %collective-permute-start.21 = (f32[1,32,128]{2,1,0:T(8,128)S(1)}, f32[1,32,128]{2,1,0:T(8,128)S(1)}, u32[]{:S(2)}, u32[]{:S(2)}) collective-permute-start(f32[1,32,128]{2,1,0:T(8,128)S(1)} %get-tuple-element.83), channel_id=1, source_target_pairs={{0,8},{8,16},{16,24},{24,32},{32,40},{40,48},{48,56},{56,64},{64,7... | collective-permute-start | bytes 49160 | tf_op jit(solution)/shard_map/ppermute | solution.py:16
  19.0 84.0 %copy-start.7 = (f32[8,32,128]{2,1,0:T(8,128)}, f32[8,32,128]{2,1,0:T(8,128)S(1)}, u32[]{:S(2)}) copy-start(f32[8,32,128]{2,1,0:T(8,128)S(1)} %get-tuple-element.61) | copy-start | bytes 393220
  19.0 84.0 %copy-start.9 = (f32[8,32,128]{2,1,0:T(8,128)}, f32[8,32,128]{2,1,0:T(8,128)S(1)}, u32[]{:S(2)}) copy-start(f32[8,32,128]{2,1,0:T(8,128)S(1)} %get-tuple-element.62) | copy-start | bytes 393220
  19.0 84.0 %copy-start.11 = (f32[8,32,128]{2,1,0:T(8,128)}, f32[8,32,128]{2,1,0:T(8,128)S(1)}, u32[]{:S(2)}) copy-start(f32[8,32,128]{2,1,0:T(8,128)S(1)} %get-tuple-element.63) | copy-start | bytes 393220
  47.4 39.9 %collective-permute-start.20 = (f32[1,32,128]{2,1,0:T(8,128)S(1)}, f32[1,32,128]{2,1,0:T(8,128)S(1)}, u32[]{:S(2)}, u32[]{:S(2)}) collective-permute-start(f32[1,32,128]{2,1,0:T(8,128)S(1)} %get-tuple-element.82), channel_id=1, source_target_pairs={{8,0},{16,8},{24,16},{32,24},{40,32},{48,40},{56,48},{64,56},{72,6... | collective-permute-start | bytes 49160 | tf_op jit(solution)/shard_map/ppermute | solution.py:19
  50.5 5.7 %collective-permute-start.2 = (f32[5,10,1,128]{3,0,2,1:T(8,128)S(1)}, f32[5,10,1,128]{3,0,2,1:T(8,128)S(1)}, u32[]{:S(2)}, u32[]{:S(2)}) collective-permute-start(f32[5,10,1,128]{3,0,2,1:T(8,128)S(1)} %get-tuple-element.49), channel_id=1, source_target_pairs={{1,0},{2,1},{3,2},{4,3},{5,4},{6,5},{7,6},{9,8},{10,9},{11,10},{12... | collective-permute-start | bytes 76808 | tf_op jit(solution)/shard_map/ppermute | solution.py:19
  51.8 8.1 %collective-permute-start.3 = (f32[5,10,1,128]{3,0,2,1:T(8,128)S(1)}, f32[5,10,1,128]{3,0,2,1:T(8,128)S(1)}, u32[]{:S(2)}, u32[]{:S(2)}) collective-permute-start(f32[5,10,1,128]{3,0,2,1:T(8,128)S(1)} %get-tuple-element.48), channel_id=1, source_target_pairs={{0,1},{1,2},{2,3},{3,4},{4,5},{5,6},{6,7},{8,9},{9,10},{10,11},{11... | collective-permute-start | bytes 76808 | tf_op jit(solution)/shard_map/ppermute | solution.py:16
  54.8 52.3 %collective-permute-start.18 = (f32[18,1,128]{2,1,0:T(1,128)S(1)}, f32[18,1,128]{2,1,0:T(1,128)S(1)}, u32[]{:S(2)}, u32[]{:S(2)}) collective-permute-start(f32[18,1,128]{2,1,0:T(1,128)S(1)} %get-tuple-element.71), channel_id=1, source_target_pairs={{1,0},{2,1},{3,2},{4,3},{5,4},{6,5},{7,6},{9,8},{10,9},{11,10},{12... | collective-permute-start | bytes 27656 | tf_op jit(solution)/shard_map/ppermute | solution.py:19
  56.2 54.9 %collective-permute-start.19 = (f32[18,1,128]{2,1,0:T(1,128)S(1)}, f32[18,1,128]{2,1,0:T(1,128)S(1)}, u32[]{:S(2)}, u32[]{:S(2)}) collective-permute-start(f32[18,1,128]{2,1,0:T(1,128)S(1)} %get-tuple-element.70), channel_id=1, source_target_pairs={{0,1},{1,2},{2,3},{3,4},{4,5},{5,6},{6,7},{8,9},{9,10},{10,11},{11... | collective-permute-start | bytes 27656 | tf_op jit(solution)/shard_map/ppermute | solution.py:16
  63.4 7.5 %collective-permute-start.4 = (f32[5,1,32,128]{3,0,2,1:T(8,128)S(1)}, f32[5,1,32,128]{3,0,2,1:T(8,128)S(1)}, u32[]{:S(2)}, u32[]{:S(2)}) collective-permute-start(f32[5,1,32,128]{3,0,2,1:T(8,128)S(1)} %get-tuple-element.57), channel_id=1, source_target_pairs={{8,0},{16,8},{24,16},{32,24},{40,32},{48,40},{56,48},{64,56},{72,6... | collective-permute-start | bytes 245768 | tf_op jit(solution)/shard_map/ppermute | solution.py:19
  65.4 7.5 %collective-permute-start.5 = (f32[5,1,32,128]{3,0,2,1:T(8,128)S(1)}, f32[5,1,32,128]{3,0,2,1:T(8,128)S(1)}, u32[]{:S(2)}, u32[]{:S(2)}) collective-permute-start(f32[5,1,32,128]{3,0,2,1:T(8,128)S(1)} %get-tuple-element.56), channel_id=1, source_target_pairs={{0,8},{8,16},{16,24},{24,32},{32,40},{40,48},{48,56},{56,64},{64,7... | collective-permute-start | bytes 245768 | tf_op jit(solution)/shard_map/ppermute | solution.py:16
  72.9 4.4 %collective-permute-start.6 = (f32[5,10,1,128]{3,0,2,1:T(8,128)S(1)}, f32[5,10,1,128]{3,0,2,1:T(8,128)S(1)}, u32[]{:S(2)}, u32[]{:S(2)}) collective-permute-start(f32[5,10,1,128]{3,0,2,1:T(8,128)S(1)} %get-tuple-element.47), channel_id=1, source_target_pairs={{1,0},{2,1},{3,2},{4,3},{5,4},{6,5},{7,6},{9,8},{10,9},{11,10},{12... | collective-permute-start | bytes 76808 | tf_op jit(solution)/shard_map/ppermute | solution.py:19
  74.2 3.9 %collective-permute-start.7 = (f32[5,10,1,128]{3,0,2,1:T(8,128)S(1)}, f32[5,10,1,128]{3,0,2,1:T(8,128)S(1)}, u32[]{:S(2)}, u32[]{:S(2)}) collective-permute-start(f32[5,10,1,128]{3,0,2,1:T(8,128)S(1)} %get-tuple-element.46), channel_id=1, source_target_pairs={{0,1},{1,2},{2,3},{3,4},{4,5},{5,6},{6,7},{8,9},{9,10},{10,11},{11... | collective-permute-start | bytes 76808 | tf_op jit(solution)/shard_map/ppermute | solution.py:16
  81.2 7.5 %collective-permute-start.8 = (f32[5,1,32,128]{3,0,2,1:T(8,128)S(1)}, f32[5,1,32,128]{3,0,2,1:T(8,128)S(1)}, u32[]{:S(2)}, u32[]{:S(2)}) collective-permute-start(f32[5,1,32,128]{3,0,2,1:T(8,128)S(1)} %get-tuple-element.55), channel_id=1, source_target_pairs={{8,0},{16,8},{24,16},{32,24},{40,32},{48,40},{56,48},{64,56},{72,6... | collective-permute-start | bytes 245768 | tf_op jit(solution)/shard_map/ppermute | solution.py:19
  83.1 7.4 %collective-permute-start.9 = (f32[5,1,32,128]{3,0,2,1:T(8,128)S(1)}, f32[5,1,32,128]{3,0,2,1:T(8,128)S(1)}, u32[]{:S(2)}, u32[]{:S(2)}) collective-permute-start(f32[5,1,32,128]{3,0,2,1:T(8,128)S(1)} %get-tuple-element.54), channel_id=1, source_target_pairs={{0,8},{8,16},{16,24},{24,32},{32,40},{40,48},{48,56},{56,64},{64,7... | collective-permute-start | bytes 245768 | tf_op jit(solution)/shard_map/ppermute | solution.py:16
  90.5 6.0 %collective-permute-start.10 = (f32[5,10,1,128]{3,0,2,1:T(8,128)S(1)}, f32[5,10,1,128]{3,0,2,1:T(8,128)S(1)}, u32[]{:S(2)}, u32[]{:S(2)}) collective-permute-start(f32[5,10,1,128]{3,0,2,1:T(8,128)S(1)} %get-tuple-element.45), channel_id=1, source_target_pairs={{1,0},{2,1},{3,2},{4,3},{5,4},{6,5},{7,6},{9,8},{10,9},{11,10},{12... | collective-permute-start | bytes 76808 | tf_op jit(solution)/shard_map/ppermute | solution.py:19
  91.8 10.4 %collective-permute-start.11 = (f32[5,10,1,128]{3,0,2,1:T(8,128)S(1)}, f32[5,10,1,128]{3,0,2,1:T(8,128)S(1)}, u32[]{:S(2)}, u32[]{:S(2)}) collective-permute-start(f32[5,10,1,128]{3,0,2,1:T(8,128)S(1)} %get-tuple-element.44), channel_id=1, source_target_pairs={{0,1},{1,2},{2,3},{3,4},{4,5},{5,6},{6,7},{8,9},{9,10},{10,11},{11... | collective-permute-start | bytes 76808 | tf_op jit(solution)/shard_map/ppermute | solution.py:16
  95.2 24.1 %collective-permute-start.22 = (f32[18,1,128]{2,1,0:T(1,128)S(1)}, f32[18,1,128]{2,1,0:T(1,128)S(1)}, u32[]{:S(2)}, u32[]{:S(2)}) collective-permute-start(f32[18,1,128]{2,1,0:T(1,128)S(1)} %get-tuple-element.73), channel_id=1, source_target_pairs={{1,0},{2,1},{3,2},{4,3},{5,4},{6,5},{7,6},{9,8},{10,9},{11,10},{12... | collective-permute-start | bytes 27656 | tf_op jit(solution)/shard_map/ppermute | solution.py:19
  96.5 22.8 %collective-permute-start.23 = (f32[18,1,128]{2,1,0:T(1,128)S(1)}, f32[18,1,128]{2,1,0:T(1,128)S(1)}, u32[]{:S(2)}, u32[]{:S(2)}) collective-permute-start(f32[18,1,128]{2,1,0:T(1,128)S(1)} %get-tuple-element.72), channel_id=1, source_target_pairs={{0,1},{1,2},{2,3},{3,4},{4,5},{5,6},{6,7},{8,9},{9,10},{10,11},{11... | collective-permute-start | bytes 27656 | tf_op jit(solution)/shard_map/ppermute | solution.py:16
  105.2 7.2 %collective-permute-start.12 = (f32[5,1,32,128]{3,0,2,1:T(8,128)S(1)}, f32[5,1,32,128]{3,0,2,1:T(8,128)S(1)}, u32[]{:S(2)}, u32[]{:S(2)}) collective-permute-start(f32[5,1,32,128]{3,0,2,1:T(8,128)S(1)} %get-tuple-element.53), channel_id=1, source_target_pairs={{8,0},{16,8},{24,16},{32,24},{40,32},{48,40},{56,48},{64,56},{72,6... | collective-permute-start | bytes 245768 | tf_op jit(solution)/shard_map/ppermute | solution.py:19
  107.2 7.5 %collective-permute-start.13 = (f32[5,1,32,128]{3,0,2,1:T(8,128)S(1)}, f32[5,1,32,128]{3,0,2,1:T(8,128)S(1)}, u32[]{:S(2)}, u32[]{:S(2)}) collective-permute-start(f32[5,1,32,128]{3,0,2,1:T(8,128)S(1)} %get-tuple-element.52), channel_id=1, source_target_pairs={{0,8},{8,16},{16,24},{24,32},{32,40},{40,48},{48,56},{56,64},{64,7... | collective-permute-start | bytes 245768 | tf_op jit(solution)/shard_map/ppermute | solution.py:16
  114.7 4.9 %collective-permute-start.14 = (f32[5,10,1,128]{3,0,2,1:T(8,128)S(1)}, f32[5,10,1,128]{3,0,2,1:T(8,128)S(1)}, u32[]{:S(2)}, u32[]{:S(2)}) collective-permute-start(f32[5,10,1,128]{3,0,2,1:T(8,128)S(1)} %get-tuple-element.43), channel_id=1, source_target_pairs={{1,0},{2,1},{3,2},{4,3},{5,4},{6,5},{7,6},{9,8},{10,9},{11,10},{12... | collective-permute-start | bytes 76808 | tf_op jit(solution)/shard_map/ppermute | solution.py:19
  116.2 3.9 %collective-permute-start.15 = (f32[5,10,1,128]{3,0,2,1:T(8,128)S(1)}, f32[5,10,1,128]{3,0,2,1:T(8,128)S(1)}, u32[]{:S(2)}, u32[]{:S(2)}) collective-permute-start(f32[5,10,1,128]{3,0,2,1:T(8,128)S(1)} %get-tuple-element.42), channel_id=1, source_target_pairs={{0,1},{1,2},{2,3},{3,4},{4,5},{5,6},{6,7},{8,9},{9,10},{10,11},{11... | collective-permute-start | bytes 76808 | tf_op jit(solution)/shard_map/ppermute | solution.py:16
  121.0 61.6 %copy-start.2 = (f32[16,32,128]{2,1,0:T(8,128)S(1)}, f32[16,32,128]{2,1,0:T(8,128)}, u32[]{:S(2)}) copy-start(f32[16,32,128]{2,1,0:T(8,128)} %param.23) | copy-start | bytes 786436
  184.0 5.9 %collective-permute-start.24 = (f32[1,32,128]{2,1,0:T(8,128)S(1)}, f32[1,32,128]{2,1,0:T(8,128)S(1)}, u32[]{:S(2)}, u32[]{:S(2)}) collective-permute-start(f32[1,32,128]{2,1,0:T(8,128)S(1)} %get-tuple-element.79), channel_id=1, source_target_pairs={{8,0},{16,8},{24,16},{32,24},{40,32},{48,40},{56,48},{64,56},{72,6... | collective-permute-start | bytes 49160 | tf_op jit(solution)/shard_map/ppermute | solution.py:19
  186.0 5.6 %collective-permute-start.25 = (f32[1,32,128]{2,1,0:T(8,128)S(1)}, f32[1,32,128]{2,1,0:T(8,128)S(1)}, u32[]{:S(2)}, u32[]{:S(2)}) collective-permute-start(f32[1,32,128]{2,1,0:T(8,128)S(1)} %get-tuple-element.78), channel_id=1, source_target_pairs={{0,8},{8,16},{16,24},{24,32},{32,40},{40,48},{48,56},{56,64},{64,7... | collective-permute-start | bytes 49160 | tf_op jit(solution)/shard_map/ppermute | solution.py:16
  191.6 4.3 %collective-permute-start.26 = (f32[18,1,128]{2,1,0:T(1,128)S(1)}, f32[18,1,128]{2,1,0:T(1,128)S(1)}, u32[]{:S(2)}, u32[]{:S(2)}) collective-permute-start(f32[18,1,128]{2,1,0:T(1,128)S(1)} %get-tuple-element.69), channel_id=1, source_target_pairs={{1,0},{2,1},{3,2},{4,3},{5,4},{6,5},{7,6},{9,8},{10,9},{11,10},{12... | collective-permute-start | bytes 27656 | tf_op jit(solution)/shard_map/ppermute | solution.py:19
  192.9 3.9 %collective-permute-start.27 = (f32[18,1,128]{2,1,0:T(1,128)S(1)}, f32[18,1,128]{2,1,0:T(1,128)S(1)}, u32[]{:S(2)}, u32[]{:S(2)}) collective-permute-start(f32[18,1,128]{2,1,0:T(1,128)S(1)} %get-tuple-element.68), channel_id=1, source_target_pairs={{0,1},{1,2},{2,3},{3,4},{4,5},{5,6},{6,7},{8,9},{9,10},{10,11},{11... | collective-permute-start | bytes 27656 | tf_op jit(solution)/shard_map/ppermute | solution.py:16
  197.5 5.9 %collective-permute-start.28 = (f32[1,32,128]{2,1,0:T(8,128)S(1)}, f32[1,32,128]{2,1,0:T(8,128)S(1)}, u32[]{:S(2)}, u32[]{:S(2)}) collective-permute-start(f32[1,32,128]{2,1,0:T(8,128)S(1)} %get-tuple-element.77), channel_id=1, source_target_pairs={{8,0},{16,8},{24,16},{32,24},{40,32},{48,40},{56,48},{64,56},{72,6... | collective-permute-start | bytes 49160 | tf_op jit(solution)/shard_map/ppermute | solution.py:19
  199.4 5.6 %collective-permute-start.29 = (f32[1,32,128]{2,1,0:T(8,128)S(1)}, f32[1,32,128]{2,1,0:T(8,128)S(1)}, u32[]{:S(2)}, u32[]{:S(2)}) collective-permute-start(f32[1,32,128]{2,1,0:T(8,128)S(1)} %get-tuple-element.76), channel_id=1, source_target_pairs={{0,8},{8,16},{16,24},{24,32},{32,40},{40,48},{48,56},{56,64},{64,7... | collective-permute-start | bytes 49160 | tf_op jit(solution)/shard_map/ppermute | solution.py:16
  205.1 6.4 %collective-permute-start.30 = (f32[18,1,128]{2,1,0:T(1,128)S(1)}, f32[18,1,128]{2,1,0:T(1,128)S(1)}, u32[]{:S(2)}, u32[]{:S(2)}) collective-permute-start(f32[18,1,128]{2,1,0:T(1,128)S(1)} %get-tuple-element.67), channel_id=1, source_target_pairs={{1,0},{2,1},{3,2},{4,3},{5,4},{6,5},{7,6},{9,8},{10,9},{11,10},{12... | collective-permute-start | bytes 27656 | tf_op jit(solution)/shard_map/ppermute | solution.py:19
  206.4 5.9 %collective-permute-start.31 = (f32[18,1,128]{2,1,0:T(1,128)S(1)}, f32[18,1,128]{2,1,0:T(1,128)S(1)}, u32[]{:S(2)}, u32[]{:S(2)}) collective-permute-start(f32[18,1,128]{2,1,0:T(1,128)S(1)} %get-tuple-element.66), channel_id=1, source_target_pairs={{0,1},{1,2},{2,3},{3,4},{4,5},{5,6},{6,7},{8,9},{9,10},{10,11},{11... | collective-permute-start | bytes 27656 | tf_op jit(solution)/shard_map/ppermute | solution.py:16
  213.1 6.2 %collective-permute-start.32 = (f32[1,32,128]{2,1,0:T(8,128)S(1)}, f32[1,32,128]{2,1,0:T(8,128)S(1)}, u32[]{:S(2)}, u32[]{:S(2)}) collective-permute-start(f32[1,32,128]{2,1,0:T(8,128)S(1)} %get-tuple-element.75), channel_id=1, source_target_pairs={{8,0},{16,8},{24,16},{32,24},{40,32},{48,40},{56,48},{64,56},{72,6... | collective-permute-start | bytes 49160 | tf_op jit(solution)/shard_map/ppermute | solution.py:19
  215.0 5.6 %collective-permute-start.33 = (f32[1,32,128]{2,1,0:T(8,128)S(1)}, f32[1,32,128]{2,1,0:T(8,128)S(1)}, u32[]{:S(2)}, u32[]{:S(2)}) collective-permute-start(f32[1,32,128]{2,1,0:T(8,128)S(1)} %get-tuple-element.74), channel_id=1, source_target_pairs={{0,8},{8,16},{16,24},{24,32},{32,40},{40,48},{48,56},{56,64},{64,7... | collective-permute-start | bytes 49160 | tf_op jit(solution)/shard_map/ppermute | solution.py:16
  220.7 6.1 %collective-permute-start.34 = (f32[18,1,128]{2,1,0:T(1,128)S(1)}, f32[18,1,128]{2,1,0:T(1,128)S(1)}, u32[]{:S(2)}, u32[]{:S(2)}) collective-permute-start(f32[18,1,128]{2,1,0:T(1,128)S(1)} %get-tuple-element.65), channel_id=1, source_target_pairs={{1,0},{2,1},{3,2},{4,3},{5,4},{6,5},{7,6},{9,8},{10,9},{11,10},{12... | collective-permute-start | bytes 27656 | tf_op jit(solution)/shard_map/ppermute | solution.py:19
  222.0 5.6 %collective-permute-start.35 = (f32[18,1,128]{2,1,0:T(1,128)S(1)}, f32[18,1,128]{2,1,0:T(1,128)S(1)}, u32[]{:S(2)}, u32[]{:S(2)}) collective-permute-start(f32[18,1,128]{2,1,0:T(1,128)S(1)} %get-tuple-element.64), channel_id=1, source_target_pairs={{0,1},{1,2},{2,3},{3,4},{4,5},{5,6},{6,7},{8,9},{9,10},{10,11},{11... | collective-permute-start | bytes 27656 | tf_op jit(solution)/shard_map/ppermute | solution.py:16
  228.9 141.1 %copy-start.19 = (f32[6]{0:T(128)S(1)}, f32[6]{0:T(128)}, u32[]{:S(2)}) copy-start(f32[6]{0:T(128)} %constant.130) | copy-start | bytes 76
  318.9 51.6 %copy-start.6 = (f32[16,32,128]{2,1,0:T(8,128)}, f32[16,32,128]{2,1,0:T(8,128)S(1)}, u32[]{:S(2)}) copy-start(f32[16,32,128]{2,1,0:T(8,128)S(1)} %divide_add_fusion) | copy-start | bytes 786436
  (8 other events, 83.2 us)
where the time goes:
time: 372 us; the launch traced here: 370 us
  blocking collectives  224 us (60%)
  starting transfers between devices  99.9 us (27%)
  waiting for transfers between devices  18.5 us (5%)
  matrix products  10.4 us (3%)
  other arithmetic  8.88 us (2%)
  local copies, waits for them, and re-layouts  6.83 us (2%)
    psum x1, blocking collectives, shards(): lax.psum(jnp.concatenate([fluid_squares, solid_squares]), ('blk', 'span'))  89.1 us
    ppermute x18, starting transfers between devices, padded(): lax.ppermute(lax.slice_in_dim(block, block.shape[dim] - width, None, axis...  69.2 us
    all_gather x1, blocking collectives, shards(): arrived = lax.all_gather(wall_flux, 'blk', axis=0, tiled=True)  59.1 us
    all_gather x1, blocking collectives, shards(): lax.all_gather(interface_heat_level, 'blk', axis=0, tiled=True)  49.3 us
    ppermute x18, starting transfers between devices, padded(): lax.ppermute(lax.slice_in_dim(block, 0, width, axis=dim), axis, backward)  30.7 us
    unnamed x1, blocking collectives  26.2 us
    ppermute x18, waiting for transfers between devices, padded(): lax.ppermute(lax.slice_in_dim(block, block.shape[dim] - width, None, axis...  14.4 us
    dot_general x4, matrix products, fluid_operator(): jnp.einsum('fg,gxyz->fxyz', jacobian, centre, precision=lax.Precision.HIG...  9.52 us
  transfers between devices with their start and end apart: 36, of which 14 were waited for; matrix products, arithmetic and copies ran while one was open for 4% of the time, Pallas kernels for 0%

commit v1 on v0

--- a/solution.py
+++ b/solution.py
@@ -144,7 +144,10 @@
             thermal_state_grid + damping_weight * metal_imbalance_grid / metal_pivot_entries
         )
     interface_heat_level = thermal_state_grid[-1]
-    boundary_patches_finished = lax.all_gather(interface_heat_level, "blk", axis=0, tiled=True)
+    boundary_patches_finished = jnp.concatenate(
+        lax.all_to_all(jnp.stack([interface_heat_level] * lax.axis_size("blk")), "blk", 0, 0),
+        axis=0,
+    )
     output_entries = jnp.take(boundary_patches_finished, owner_local * rows + target_local, axis=0)
     gas_outcome = adjoint.at[4, 0].add(wall_coefficient[0] * output_entries)
     solid_squares = jnp.sum(metal_imbalance_grid * metal_imbalance_grid)[None]

time: 372 us -> 334 us (0.90)
  blocking collectives: 224 us -> 166 us
  starting transfers between devices: 99.9 us -> 119 us
    all_gather x1 -> x0, blocking collectives: 49.3 us -> none  [shards(): lax.all_gather(interface_heat_level, 'blk', axis=0, tiled=True)]
    all_to_all x0 -> x1, starting transfers between devices: none -> 18.7 us  [shards(): lax.all_to_all(jnp.stack([interface_heat_level] * lax.axis_size('blk')),...]
    psum x1, blocking collectives: 89.1 us -> 80.8 us  [shards(): lax.psum(jnp.concatenate([fluid_squares, solid_squares]), ('blk', 'span'))]
  transfers between devices with their start and end apart: 36 -> 37, of which waited for: 14 -> 14; matrix products, arithmetic and copies ran while one was open for 4% -> 4% of each run, Pallas kernels for 0% -> 0%
where the time goes in v1:
time: 334 us; the launch traced here: 331 us
  blocking collectives  166 us (50%)
  starting transfers between devices  119 us (36%)
  waiting for transfers between devices  18.3 us (5%)
  matrix products  10 us (3%)
  other arithmetic  8.9 us (3%)
  local copies, waits for them, and re-layouts  6.96 us (2%)
    psum x1, blocking collectives, shards(): lax.psum(jnp.concatenate([fluid_squares, solid_squares]), ('blk', 'span'))  80.8 us
    ppermute x18, starting transfers between devices, padded(): lax.ppermute(lax.slice_in_dim(block, block.shape[dim] - width, None, axis...  69.4 us
    all_gather x1, blocking collectives, shards(): arrived = lax.all_gather(wall_flux, 'blk', axis=0, tiled=True)  59.1 us
    ppermute x18, starting transfers between devices, padded(): lax.ppermute(lax.slice_in_dim(block, 0, width, axis=dim), axis, backward)  30.6 us
    unnamed x1, blocking collectives  26.2 us
    all_to_all x1, starting transfers between devices, shards(): lax.all_to_all(jnp.stack([interface_heat_level] * lax.axis_size('blk')),...  18.7 us
    ppermute x18, waiting for transfers between devices, padded(): lax.ppermute(lax.slice_in_dim(block, block.shape[dim] - width, None, axis...  14.3 us
    dot_general x4, matrix products, fluid_operator(): jnp.einsum('fg,gxyz->fxyz', jacobian, centre, precision=lax.Precision.HIG...  9.13 us
  transfers between devices with their start and end apart: 37, of which 14 were waited for; matrix products, arithmetic and copies ran while one was open for 4% of the time, Pallas kernels for 0%

profile of v1, /device:TPU:2, one launch (start us, length us, event | category | flops | bytes accessed | tf_op | source)
XLA Modules:
  0.0 331.3 jit_solution(13422069845040126709)
XLA Ops:
  0.7 1.6 copy.36
  2.4 3.4 %collective-permute-start.1 = (f32[5,1,32,128]{3,0,2,1:T(8,128)S(1)}, f32[5,1,32,128]{3,0,2,1:T(8,128)S(1)}, u32[]{:S(2)}, u32[]{:S(2)}) collective-permute-start(f32[5,1,32,128]{3,0,2,1:T(8,128)S(1)} %get-tuple-element.59), channel_id=1, source_target_pairs={{0,8},{8,16},{16,24},{24,32},{32,40},{40,48},{48,56},{56,64},{64,7... | collective-permute-start | bytes 245768 | tf_op jit(solution)/shard_map/ppermute | solution.py:16
  5.8 2.4 collective-permute-start
  9.0 3.4 %collective-permute-start.17 = (f32[1,32,128]{2,1,0:T(8,128)S(1)}, f32[1,32,128]{2,1,0:T(8,128)S(1)}, u32[]{:S(2)}, u32[]{:S(2)}) collective-permute-start(f32[1,32,128]{2,1,0:T(8,128)S(1)} %get-tuple-element.80), channel_id=1, source_target_pairs={{0,8},{8,16},{16,24},{24,32},{32,40},{40,48},{48,56},{56,64},{64,7... | collective-permute-start | bytes 49160 | tf_op jit(solution)/shard_map/ppermute | solution.py:16
  12.3 2.4 collective-permute-start.16
  14.8 3.4 %collective-permute-start.21 = (f32[1,32,128]{2,1,0:T(8,128)S(1)}, f32[1,32,128]{2,1,0:T(8,128)S(1)}, u32[]{:S(2)}, u32[]{:S(2)}) collective-permute-start(f32[1,32,128]{2,1,0:T(8,128)S(1)} %get-tuple-element.83), channel_id=1, source_target_pairs={{0,8},{8,16},{16,24},{24,32},{32,40},{40,48},{48,56},{56,64},{64,7... | collective-permute-start | bytes 49160 | tf_op jit(solution)/shard_map/ppermute | solution.py:16
  19.8 26.2 %all-reduce.11 = (s32[1024]{0:T(1024)S(1)}, s32[1024]{0:T(1024)S(1)}) all-reduce(s32[1024]{0:T(1024)S(1)} %bitcast_dynamic-update-slice_fusion.1, s32[1024]{0:T(1024)S(1)} %bitcast_dynamic-update-slice_fusion), channel_id=2, replica_groups=mesh['blk'=32,'span'=8] {'blk'}, use_global_device_ids=true, to_apply=%add.9 | all-reduce | flops 2048 | bytes 16384
  46.7 2.5 collective-permute-start.20
  49.8 1.3 collective-permute-start.2
  51.1 3.0 collective-permute-start.3
  55.4 3.7 %collective-permute-start.19 = (f32[18,1,128]{2,1,0:T(1,128)S(1)}, f32[18,1,128]{2,1,0:T(1,128)S(1)}, u32[]{:S(2)}, u32[]{:S(2)}) collective-permute-start(f32[18,1,128]{2,1,0:T(1,128)S(1)} %get-tuple-element.70), channel_id=1, source_target_pairs={{0,1},{1,2},{2,3},{3,4},{4,5},{5,6},{6,7},{8,9},{9,10},{10,11},{11... | collective-permute-start | bytes 27656 | tf_op jit(solution)/shard_map/ppermute | solution.py:16
  60.0 2.6 fusion.10
  62.6 1.9 collective-permute-start.4
  64.6 3.9 %collective-permute-start.5 = (f32[5,1,32,128]{3,0,2,1:T(8,128)S(1)}, f32[5,1,32,128]{3,0,2,1:T(8,128)S(1)}, u32[]{:S(2)}, u32[]{:S(2)}) collective-permute-start(f32[5,1,32,128]{3,0,2,1:T(8,128)S(1)} %get-tuple-element.56), channel_id=1, source_target_pairs={{0,8},{8,16},{16,24},{24,32},{32,40},{40,48},{48,56},{56,64},{64,7... | collective-permute-start | bytes 245768 | tf_op jit(solution)/shard_map/ppermute | solution.py:16
  68.5 1.6 collective-permute-done.4
  70.2 1.9 collective-permute-done.5
  72.1 1.3 collective-permute-start.6
  73.4 3.1 collective-permute-start.7
  78.2 2.1 fusion.11
  80.3 1.9 collective-permute-start.8
  82.2 4.2 %collective-permute-start.9 = (f32[5,1,32,128]{3,0,2,1:T(8,128)S(1)}, f32[5,1,32,128]{3,0,2,1:T(8,128)S(1)}, u32[]{:S(2)}, u32[]{:S(2)}) collective-permute-start(f32[5,1,32,128]{3,0,2,1:T(8,128)S(1)} %get-tuple-element.54), channel_id=1, source_target_pairs={{0,8},{8,16},{16,24},{24,32},{32,40},{40,48},{48,56},{56,64},{64,7... | collective-permute-start | bytes 245768 | tf_op jit(solution)/shard_map/ppermute | solution.py:16
  86.4 1.4 collective-permute-done.8
  87.8 1.8 collective-permute-done.9
  90.9 3.4 %collective-permute-start.11 = (f32[5,10,1,128]{3,0,2,1:T(8,128)S(1)}, f32[5,10,1,128]{3,0,2,1:T(8,128)S(1)}, u32[]{:S(2)}, u32[]{:S(2)}) collective-permute-start(f32[5,10,1,128]{3,0,2,1:T(8,128)S(1)} %get-tuple-element.44), channel_id=1, source_target_pairs={{0,1},{1,2},{2,3},{3,4},{4,5},{5,6},{6,7},{8,9},{9,10},{10,11},{11... | collective-permute-start | bytes 76808 | tf_op jit(solution)/shard_map/ppermute | solution.py:16
  94.2 1.3 collective-permute-start.22
  95.5 5.7 %collective-permute-start.23 = (f32[18,1,128]{2,1,0:T(1,128)S(1)}, f32[18,1,128]{2,1,0:T(1,128)S(1)}, u32[]{:S(2)}, u32[]{:S(2)}) collective-permute-start(f32[18,1,128]{2,1,0:T(1,128)S(1)} %get-tuple-element.72), channel_id=1, source_target_pairs={{0,1},{1,2},{2,3},{3,4},{4,5},{5,6},{6,7},{8,9},{9,10},{10,11},{11... | collective-permute-start | bytes 27656 | tf_op jit(solution)/shard_map/ppermute | solution.py:16
  102.1 2.1 fusion.12
  104.2 1.9 collective-permute-start.12
  106.1 3.9 %collective-permute-start.13 = (f32[5,1,32,128]{3,0,2,1:T(8,128)S(1)}, f32[5,1,32,128]{3,0,2,1:T(8,128)S(1)}, u32[]{:S(2)}, u32[]{:S(2)}) collective-permute-start(f32[5,1,32,128]{3,0,2,1:T(8,128)S(1)} %get-tuple-element.52), channel_id=1, source_target_pairs={{0,8},{8,16},{16,24},{24,32},{32,40},{40,48},{48,56},{56,64},{64,7... | collective-permute-start | bytes 245768 | tf_op jit(solution)/shard_map/ppermute | solution.py:16
  111.4 2.3 collective-permute-done.13
  114.9 3.1 collective-permute-start.15
  119.7 2.4 multiply_reduce_fusion
  122.2 59.1 %all_gather.11 = f32[1024,128]{1,0:T(8,128)S(1)} all-gather(f32[32,128]{1,0:T(8,128)S(1)} %bitcast_multiply_fusion), channel_id=1, replica_groups=mesh['blk'=32,'span'=8] {'blk'}, dimensions={0}, use_global_device_ids=true | all-gather | bytes 540672 | tf_op jit(solution)/shard_map/all_gather | solution.py:129
  182.7 1.9 collective-permute-start.24
  184.7 3.9 %collective-permute-start.25 = (f32[1,32,128]{2,1,0:T(8,128)S(1)}, f32[1,32,128]{2,1,0:T(8,128)S(1)}, u32[]{:S(2)}, u32[]{:S(2)}) collective-permute-start(f32[1,32,128]{2,1,0:T(8,128)S(1)} %get-tuple-element.78), channel_id=1, source_target_pairs={{0,8},{8,16},{16,24},{24,32},{32,40},{40,48},{48,56},{56,64},{64,7... | collective-permute-start | bytes 49160 | tf_op jit(solution)/shard_map/ppermute | solution.py:16
  188.6 1.7 collective-permute-done.25
  190.3 1.3 collective-permute-start.26
  191.6 3.0 collective-permute-start.27
  196.2 1.9 collective-permute-start.28
  198.1 3.9 %collective-permute-start.29 = (f32[1,32,128]{2,1,0:T(8,128)S(1)}, f32[1,32,128]{2,1,0:T(8,128)S(1)}, u32[]{:S(2)}, u32[]{:S(2)}) collective-permute-start(f32[1,32,128]{2,1,0:T(8,128)S(1)} %get-tuple-element.76), channel_id=1, source_target_pairs={{0,8},{8,16},{16,24},{24,32},{32,40},{40,48},{48,56},{56,64},{64,7... | collective-permute-start | bytes 49160 | tf_op jit(solution)/shard_map/ppermute | solution.py:16
  202.1 1.7 collective-permute-done.29
  205.1 5.1 %collective-permute-start.31 = (f32[18,1,128]{2,1,0:T(1,128)S(1)}, f32[18,1,128]{2,1,0:T(1,128)S(1)}, u32[]{:S(2)}, u32[]{:S(2)}) collective-permute-start(f32[18,1,128]{2,1,0:T(1,128)S(1)} %get-tuple-element.66), channel_id=1, source_target_pairs={{0,1},{1,2},{2,3},{3,4},{4,5},{5,6},{6,7},{8,9},{9,10},{10,11},{11... | collective-permute-start | bytes 27656 | tf_op jit(solution)/shard_map/ppermute | solution.py:16
  211.8 1.9 collective-permute-start.32
  213.7 4.2 %collective-permute-start.33 = (f32[1,32,128]{2,1,0:T(8,128)S(1)}, f32[1,32,128]{2,1,0:T(8,128)S(1)}, u32[]{:S(2)}, u32[]{:S(2)}) collective-permute-start(f32[1,32,128]{2,1,0:T(8,128)S(1)} %get-tuple-element.74), channel_id=1, source_target_pairs={{0,8},{8,16},{16,24},{24,32},{32,40},{40,48},{48,56},{56,64},{64,7... | collective-permute-start | bytes 49160 | tf_op jit(solution)/shard_map/ppermute | solution.py:16
  217.9 1.4 collective-permute-done.33
  220.7 5.0 %collective-permute-start.35 = (f32[18,1,128]{2,1,0:T(1,128)S(1)}, f32[18,1,128]{2,1,0:T(1,128)S(1)}, u32[]{:S(2)}, u32[]{:S(2)}) collective-permute-start(f32[18,1,128]{2,1,0:T(1,128)S(1)} %get-tuple-element.64), channel_id=1, source_target_pairs={{0,1},{1,2},{2,3},{3,4},{4,5},{5,6},{6,7},{8,9},{9,10},{10,11},{11... | collective-permute-start | bytes 27656 | tf_op jit(solution)/shard_map/ppermute | solution.py:16
  228.7 18.7 %all-to-all-start = ((f32[32,32,128]{2,1,0:T(8,128)}), f32[32,32,128]{2,1,0:T(8,128)S(1)}, u32[]{:S(2)}, u32[]{:S(2)}) async-start(f32[32,32,128]{2,1,0:T(8,128)} %stack.3), calls=%async_computation | async-start | bytes 1048576 | tf_op jit(solution)/shard_map/all_to_all | solution.py:148
  248.2 80.8 %psum.7 = f32[6]{0:T(128)S(1)} all-reduce(f32[6]{0:T(128)S(1)} %pad_maximum_fusion.78), channel_id=1, replica_groups=mesh['blk'=32,'span'=8] {'blk','span'}, use_global_device_ids=true, to_apply=%region_2.3 | all-reduce | flops 6 | bytes 48 | tf_op jit(solution)/shard_map/psum | solution.py:154
  (127 shorter events, 26.1 us)
Async XLA Ops:
  0.6 45.4 %copy-start = (f32[5,5]{1,0:T(8,128)S(1)}, f32[5,5]{1,0:T(8,128)}, u32[]{:S(2)}) copy-start(f32[5,5]{1,0:T(8,128)} %param.20) | copy-start | bytes 304
  0.6 17.7 %copy-start.12 = (u32[256]{0:T(256)S(1)}, u32[256]{0:T(256)}, u32[]{:S(2)}) copy-start(u32[256]{0:T(256)} %constant.146) | copy-start | bytes 3076
  0.7 48.6 %copy-start.3 = (f32[5,8,32,128]{3,2,1,0:T(8,128)S(1)}, f32[5,8,32,128]{3,2,1,0:T(8,128)}, u32[]{:S(2)}) copy-start(f32[5,8,32,128]{3,2,1,0:T(8,128)} %param.16) | copy-start | bytes 1966084
  0.7 17.6 %copy-start.5 = (f32[3,8,32,128]{3,2,1,0:T(8,128)S(1)}, f32[3,8,32,128]{3,2,1,0:T(8,128)}, u32[]{:S(2)}) copy-start(f32[3,8,32,128]{3,2,1,0:T(8,128)} %param.18) | copy-start | bytes 1179652
  0.7 17.6 %copy-start.9 = (f32[5]{0:T(128)S(1)}, f32[5]{0:T(128)}, u32[]{:S(2)}) copy-start(f32[5]{0:T(128)} %param.19) | copy-start | bytes 64
  0.7 48.5 %copy-start.1 = (f32[16,32,128]{2,1,0:T(8,128)S(1)}, f32[16,32,128]{2,1,0:T(8,128)}, u32[]{:S(2)}) copy-start(f32[16,32,128]{2,1,0:T(8,128)} %param.24) | copy-start | bytes 786436
  0.7 18.9 %copy-start.11 = (s32[1,32,1]{1,2,0:T(1,128)S(1)}, s32[1,32,1]{1,2,0:T(1,128)}, u32[]{:S(2)}) copy-start(s32[1,32,1]{1,2,0:T(1,128)} %param.25) | copy-start | bytes 388
  0.7 19.0 %copy-start.10 = (s32[1,32]{1,0:T(1,128)S(1)}, s32[1,32]{1,0:T(1,128)}, u32[]{:S(2)}) copy-start(s32[1,32]{1,0:T(1,128)} %param.26) | copy-start | bytes 388
  2.4 46.9 %collective-permute-start.1 = (f32[5,1,32,128]{3,0,2,1:T(8,128)S(1)}, f32[5,1,32,128]{3,0,2,1:T(8,128)S(1)}, u32[]{:S(2)}, u32[]{:S(2)}) collective-permute-start(f32[5,1,32,128]{3,0,2,1:T(8,128)S(1)} %get-tuple-element.59), channel_id=1, source_target_pairs={{0,8},{8,16},{16,24},{24,32},{32,40},{40,48},{48,56},{56,64},{64,7... | collective-permute-start | bytes 245768 | tf_op jit(solution)/shard_map/ppermute | solution.py:16
  5.8 44.0 %collective-permute-start = (f32[5,1,32,128]{3,0,2,1:T(8,128)S(1)}, f32[5,1,32,128]{3,0,2,1:T(8,128)S(1)}, u32[]{:S(2)}, u32[]{:S(2)}) collective-permute-start(f32[5,1,32,128]{3,0,2,1:T(8,128)S(1)} %get-tuple-element.58), channel_id=1, source_target_pairs={{8,0},{16,8},{24,16},{32,24},{40,32},{48,40},{56,48},{64,56},{72,6... | collective-permute-start | bytes 245768 | tf_op jit(solution)/shard_map/ppermute | solution.py:19
  9.0 37.7 %collective-permute-start.17 = (f32[1,32,128]{2,1,0:T(8,128)S(1)}, f32[1,32,128]{2,1,0:T(8,128)S(1)}, u32[]{:S(2)}, u32[]{:S(2)}) collective-permute-start(f32[1,32,128]{2,1,0:T(8,128)S(1)} %get-tuple-element.80), channel_id=1, source_target_pairs={{0,8},{8,16},{16,24},{24,32},{32,40},{40,48},{48,56},{56,64},{64,7... | collective-permute-start | bytes 49160 | tf_op jit(solution)/shard_map/ppermute | solution.py:16
  12.3 36.9 %collective-permute-start.16 = (f32[1,32,128]{2,1,0:T(8,128)S(1)}, f32[1,32,128]{2,1,0:T(8,128)S(1)}, u32[]{:S(2)}, u32[]{:S(2)}) collective-permute-start(f32[1,32,128]{2,1,0:T(8,128)S(1)} %get-tuple-element.81), channel_id=1, source_target_pairs={{8,0},{16,8},{24,16},{32,24},{40,32},{48,40},{56,48},{64,56},{72,6... | collective-permute-start | bytes 49160 | tf_op jit(solution)/shard_map/ppermute | solution.py:19
  14.8 49.7 %collective-permute-start.21 = (f32[1,32,128]{2,1,0:T(8,128)S(1)}, f32[1,32,128]{2,1,0:T(8,128)S(1)}, u32[]{:S(2)}, u32[]{:S(2)}) collective-permute-start(f32[1,32,128]{2,1,0:T(8,128)S(1)} %get-tuple-element.83), channel_id=1, source_target_pairs={{0,8},{8,16},{16,24},{24,32},{32,40},{40,48},{48,56},{56,64},{64,7... | collective-permute-start | bytes 49160 | tf_op jit(solution)/shard_map/ppermute | solution.py:16
  46.7 39.7 %collective-permute-start.20 = (f32[1,32,128]{2,1,0:T(8,128)S(1)}, f32[1,32,128]{2,1,0:T(8,128)S(1)}, u32[]{:S(2)}, u32[]{:S(2)}) collective-permute-start(f32[1,32,128]{2,1,0:T(8,128)S(1)} %get-tuple-element.82), channel_id=1, source_target_pairs={{8,0},{16,8},{24,16},{32,24},{40,32},{48,40},{56,48},{64,56},{72,6... | collective-permute-start | bytes 49160 | tf_op jit(solution)/shard_map/ppermute | solution.py:19
  49.8 5.7 %collective-permute-start.2 = (f32[5,10,1,128]{3,0,2,1:T(8,128)S(1)}, f32[5,10,1,128]{3,0,2,1:T(8,128)S(1)}, u32[]{:S(2)}, u32[]{:S(2)}) collective-permute-start(f32[5,10,1,128]{3,0,2,1:T(8,128)S(1)} %get-tuple-element.49), channel_id=1, source_target_pairs={{1,0},{2,1},{3,2},{4,3},{5,4},{6,5},{7,6},{9,8},{10,9},{11,10},{12... | collective-permute-start | bytes 76808 | tf_op jit(solution)/shard_map/ppermute | solution.py:19
  51.1 8.1 %collective-permute-start.3 = (f32[5,10,1,128]{3,0,2,1:T(8,128)S(1)}, f32[5,10,1,128]{3,0,2,1:T(8,128)S(1)}, u32[]{:S(2)}, u32[]{:S(2)}) collective-permute-start(f32[5,10,1,128]{3,0,2,1:T(8,128)S(1)} %get-tuple-element.48), channel_id=1, source_target_pairs={{0,1},{1,2},{2,3},{3,4},{4,5},{5,6},{6,7},{8,9},{9,10},{10,11},{11... | collective-permute-start | bytes 76808 | tf_op jit(solution)/shard_map/ppermute | solution.py:16
  54.1 52.0 %collective-permute-start.18 = (f32[18,1,128]{2,1,0:T(1,128)S(1)}, f32[18,1,128]{2,1,0:T(1,128)S(1)}, u32[]{:S(2)}, u32[]{:S(2)}) collective-permute-start(f32[18,1,128]{2,1,0:T(1,128)S(1)} %get-tuple-element.71), channel_id=1, source_target_pairs={{1,0},{2,1},{3,2},{4,3},{5,4},{6,5},{7,6},{9,8},{10,9},{11,10},{12... | collective-permute-start | bytes 27656 | tf_op jit(solution)/shard_map/ppermute | solution.py:19
  55.4 54.6 %collective-permute-start.19 = (f32[18,1,128]{2,1,0:T(1,128)S(1)}, f32[18,1,128]{2,1,0:T(1,128)S(1)}, u32[]{:S(2)}, u32[]{:S(2)}) collective-permute-start(f32[18,1,128]{2,1,0:T(1,128)S(1)} %get-tuple-element.70), channel_id=1, source_target_pairs={{0,1},{1,2},{2,3},{3,4},{4,5},{5,6},{6,7},{8,9},{9,10},{10,11},{11... | collective-permute-start | bytes 27656 | tf_op jit(solution)/shard_map/ppermute | solution.py:16
  62.6 7.5 %collective-permute-start.4 = (f32[5,1,32,128]{3,0,2,1:T(8,128)S(1)}, f32[5,1,32,128]{3,0,2,1:T(8,128)S(1)}, u32[]{:S(2)}, u32[]{:S(2)}) collective-permute-start(f32[5,1,32,128]{3,0,2,1:T(8,128)S(1)} %get-tuple-element.57), channel_id=1, source_target_pairs={{8,0},{16,8},{24,16},{32,24},{40,32},{48,40},{56,48},{64,56},{72,6... | collective-permute-start | bytes 245768 | tf_op jit(solution)/shard_map/ppermute | solution.py:19
  64.6 7.5 %collective-permute-start.5 = (f32[5,1,32,128]{3,0,2,1:T(8,128)S(1)}, f32[5,1,32,128]{3,0,2,1:T(8,128)S(1)}, u32[]{:S(2)}, u32[]{:S(2)}) collective-permute-start(f32[5,1,32,128]{3,0,2,1:T(8,128)S(1)} %get-tuple-element.56), channel_id=1, source_target_pairs={{0,8},{8,16},{16,24},{24,32},{32,40},{40,48},{48,56},{56,64},{64,7... | collective-permute-start | bytes 245768 | tf_op jit(solution)/shard_map/ppermute | solution.py:16
  72.1 4.4 %collective-permute-start.6 = (f32[5,10,1,128]{3,0,2,1:T(8,128)S(1)}, f32[5,10,1,128]{3,0,2,1:T(8,128)S(1)}, u32[]{:S(2)}, u32[]{:S(2)}) collective-permute-start(f32[5,10,1,128]{3,0,2,1:T(8,128)S(1)} %get-tuple-element.47), channel_id=1, source_target_pairs={{1,0},{2,1},{3,2},{4,3},{5,4},{6,5},{7,6},{9,8},{10,9},{11,10},{12... | collective-permute-start | bytes 76808 | tf_op jit(solution)/shard_map/ppermute | solution.py:19
  73.4 4.0 %collective-permute-start.7 = (f32[5,10,1,128]{3,0,2,1:T(8,128)S(1)}, f32[5,10,1,128]{3,0,2,1:T(8,128)S(1)}, u32[]{:S(2)}, u32[]{:S(2)}) collective-permute-start(f32[5,10,1,128]{3,0,2,1:T(8,128)S(1)} %get-tuple-element.46), channel_id=1, source_target_pairs={{0,1},{1,2},{2,3},{3,4},{4,5},{5,6},{6,7},{8,9},{9,10},{10,11},{11... | collective-permute-start | bytes 76808 | tf_op jit(solution)/shard_map/ppermute | solution.py:16
  80.3 7.5 %collective-permute-start.8 = (f32[5,1,32,128]{3,0,2,1:T(8,128)S(1)}, f32[5,1,32,128]{3,0,2,1:T(8,128)S(1)}, u32[]{:S(2)}, u32[]{:S(2)}) collective-permute-start(f32[5,1,32,128]{3,0,2,1:T(8,128)S(1)} %get-tuple-element.55), channel_id=1, source_target_pairs={{8,0},{16,8},{24,16},{32,24},{40,32},{48,40},{56,48},{64,56},{72,6... | collective-permute-start | bytes 245768 | tf_op jit(solution)/shard_map/ppermute | solution.py:19
  82.2 7.4 %collective-permute-start.9 = (f32[5,1,32,128]{3,0,2,1:T(8,128)S(1)}, f32[5,1,32,128]{3,0,2,1:T(8,128)S(1)}, u32[]{:S(2)}, u32[]{:S(2)}) collective-permute-start(f32[5,1,32,128]{3,0,2,1:T(8,128)S(1)} %get-tuple-element.54), channel_id=1, source_target_pairs={{0,8},{8,16},{16,24},{24,32},{32,40},{40,48},{48,56},{56,64},{64,7... | collective-permute-start | bytes 245768 | tf_op jit(solution)/shard_map/ppermute | solution.py:16
  89.6 6.0 %collective-permute-start.10 = (f32[5,10,1,128]{3,0,2,1:T(8,128)S(1)}, f32[5,10,1,128]{3,0,2,1:T(8,128)S(1)}, u32[]{:S(2)}, u32[]{:S(2)}) collective-permute-start(f32[5,10,1,128]{3,0,2,1:T(8,128)S(1)} %get-tuple-element.45), channel_id=1, source_target_pairs={{1,0},{2,1},{3,2},{4,3},{5,4},{6,5},{7,6},{9,8},{10,9},{11,10},{12... | collective-permute-start | bytes 76808 | tf_op jit(solution)/shard_map/ppermute | solution.py:19
  90.9 10.4 %collective-permute-start.11 = (f32[5,10,1,128]{3,0,2,1:T(8,128)S(1)}, f32[5,10,1,128]{3,0,2,1:T(8,128)S(1)}, u32[]{:S(2)}, u32[]{:S(2)}) collective-permute-start(f32[5,10,1,128]{3,0,2,1:T(8,128)S(1)} %get-tuple-element.44), channel_id=1, source_target_pairs={{0,1},{1,2},{2,3},{3,4},{4,5},{5,6},{6,7},{8,9},{9,10},{10,11},{11... | collective-permute-start | bytes 76808 | tf_op jit(solution)/shard_map/ppermute | solution.py:16
  94.2 23.8 %collective-permute-start.22 = (f32[18,1,128]{2,1,0:T(1,128)S(1)}, f32[18,1,128]{2,1,0:T(1,128)S(1)}, u32[]{:S(2)}, u32[]{:S(2)}) collective-permute-start(f32[18,1,128]{2,1,0:T(1,128)S(1)} %get-tuple-element.73), channel_id=1, source_target_pairs={{1,0},{2,1},{3,2},{4,3},{5,4},{6,5},{7,6},{9,8},{10,9},{11,10},{12... | collective-permute-start | bytes 27656 | tf_op jit(solution)/shard_map/ppermute | solution.py:19
  95.5 22.5 %collective-permute-start.23 = (f32[18,1,128]{2,1,0:T(1,128)S(1)}, f32[18,1,128]{2,1,0:T(1,128)S(1)}, u32[]{:S(2)}, u32[]{:S(2)}) collective-permute-start(f32[18,1,128]{2,1,0:T(1,128)S(1)} %get-tuple-element.72), channel_id=1, source_target_pairs={{0,1},{1,2},{2,3},{3,4},{4,5},{5,6},{6,7},{8,9},{9,10},{10,11},{11... | collective-permute-start | bytes 27656 | tf_op jit(solution)/shard_map/ppermute | solution.py:16
  104.2 7.2 %collective-permute-start.12 = (f32[5,1,32,128]{3,0,2,1:T(8,128)S(1)}, f32[5,1,32,128]{3,0,2,1:T(8,128)S(1)}, u32[]{:S(2)}, u32[]{:S(2)}) collective-permute-start(f32[5,1,32,128]{3,0,2,1:T(8,128)S(1)} %get-tuple-element.53), channel_id=1, source_target_pairs={{8,0},{16,8},{24,16},{32,24},{40,32},{48,40},{56,48},{64,56},{72,6... | collective-permute-start | bytes 245768 | tf_op jit(solution)/shard_map/ppermute | solution.py:19
  106.1 7.5 %collective-permute-start.13 = (f32[5,1,32,128]{3,0,2,1:T(8,128)S(1)}, f32[5,1,32,128]{3,0,2,1:T(8,128)S(1)}, u32[]{:S(2)}, u32[]{:S(2)}) collective-permute-start(f32[5,1,32,128]{3,0,2,1:T(8,128)S(1)} %get-tuple-element.52), channel_id=1, source_target_pairs={{0,8},{8,16},{16,24},{24,32},{32,40},{40,48},{48,56},{56,64},{64,7... | collective-permute-start | bytes 245768 | tf_op jit(solution)/shard_map/ppermute | solution.py:16
  113.6 4.8 %collective-permute-start.14 = (f32[5,10,1,128]{3,0,2,1:T(8,128)S(1)}, f32[5,10,1,128]{3,0,2,1:T(8,128)S(1)}, u32[]{:S(2)}, u32[]{:S(2)}) collective-permute-start(f32[5,10,1,128]{3,0,2,1:T(8,128)S(1)} %get-tuple-element.43), channel_id=1, source_target_pairs={{1,0},{2,1},{3,2},{4,3},{5,4},{6,5},{7,6},{9,8},{10,9},{11,10},{12... | collective-permute-start | bytes 76808 | tf_op jit(solution)/shard_map/ppermute | solution.py:19
  114.9 3.9 %collective-permute-start.15 = (f32[5,10,1,128]{3,0,2,1:T(8,128)S(1)}, f32[5,10,1,128]{3,0,2,1:T(8,128)S(1)}, u32[]{:S(2)}, u32[]{:S(2)}) collective-permute-start(f32[5,10,1,128]{3,0,2,1:T(8,128)S(1)} %get-tuple-element.42), channel_id=1, source_target_pairs={{0,1},{1,2},{2,3},{3,4},{4,5},{5,6},{6,7},{8,9},{9,10},{10,11},{11... | collective-permute-start | bytes 76808 | tf_op jit(solution)/shard_map/ppermute | solution.py:16
  119.7 61.6 %copy-start.2 = (f32[16,32,128]{2,1,0:T(8,128)S(1)}, f32[16,32,128]{2,1,0:T(8,128)}, u32[]{:S(2)}) copy-start(f32[16,32,128]{2,1,0:T(8,128)} %param.23) | copy-start | bytes 786436
  182.7 5.9 %collective-permute-start.24 = (f32[1,32,128]{2,1,0:T(8,128)S(1)}, f32[1,32,128]{2,1,0:T(8,128)S(1)}, u32[]{:S(2)}, u32[]{:S(2)}) collective-permute-start(f32[1,32,128]{2,1,0:T(8,128)S(1)} %get-tuple-element.79), channel_id=1, source_target_pairs={{8,0},{16,8},{24,16},{32,24},{40,32},{48,40},{56,48},{64,56},{72,6... | collective-permute-start | bytes 49160 | tf_op jit(solution)/shard_map/ppermute | solution.py:19
  184.7 5.6 %collective-permute-start.25 = (f32[1,32,128]{2,1,0:T(8,128)S(1)}, f32[1,32,128]{2,1,0:T(8,128)S(1)}, u32[]{:S(2)}, u32[]{:S(2)}) collective-permute-start(f32[1,32,128]{2,1,0:T(8,128)S(1)} %get-tuple-element.78), channel_id=1, source_target_pairs={{0,8},{8,16},{16,24},{24,32},{32,40},{40,48},{48,56},{56,64},{64,7... | collective-permute-start | bytes 49160 | tf_op jit(solution)/shard_map/ppermute | solution.py:16
  190.3 4.3 %collective-permute-start.26 = (f32[18,1,128]{2,1,0:T(1,128)S(1)}, f32[18,1,128]{2,1,0:T(1,128)S(1)}, u32[]{:S(2)}, u32[]{:S(2)}) collective-permute-start(f32[18,1,128]{2,1,0:T(1,128)S(1)} %get-tuple-element.69), channel_id=1, source_target_pairs={{1,0},{2,1},{3,2},{4,3},{5,4},{6,5},{7,6},{9,8},{10,9},{11,10},{12... | collective-permute-start | bytes 27656 | tf_op jit(solution)/shard_map/ppermute | solution.py:19
  191.6 3.9 %collective-permute-start.27 = (f32[18,1,128]{2,1,0:T(1,128)S(1)}, f32[18,1,128]{2,1,0:T(1,128)S(1)}, u32[]{:S(2)}, u32[]{:S(2)}) collective-permute-start(f32[18,1,128]{2,1,0:T(1,128)S(1)} %get-tuple-element.68), channel_id=1, source_target_pairs={{0,1},{1,2},{2,3},{3,4},{4,5},{5,6},{6,7},{8,9},{9,10},{10,11},{11... | collective-permute-start | bytes 27656 | tf_op jit(solution)/shard_map/ppermute | solution.py:16
  196.2 5.9 %collective-permute-start.28 = (f32[1,32,128]{2,1,0:T(8,128)S(1)}, f32[1,32,128]{2,1,0:T(8,128)S(1)}, u32[]{:S(2)}, u32[]{:S(2)}) collective-permute-start(f32[1,32,128]{2,1,0:T(8,128)S(1)} %get-tuple-element.77), channel_id=1, source_target_pairs={{8,0},{16,8},{24,16},{32,24},{40,32},{48,40},{56,48},{64,56},{72,6... | collective-permute-start | bytes 49160 | tf_op jit(solution)/shard_map/ppermute | solution.py:19
  198.1 5.6 %collective-permute-start.29 = (f32[1,32,128]{2,1,0:T(8,128)S(1)}, f32[1,32,128]{2,1,0:T(8,128)S(1)}, u32[]{:S(2)}, u32[]{:S(2)}) collective-permute-start(f32[1,32,128]{2,1,0:T(8,128)S(1)} %get-tuple-element.76), channel_id=1, source_target_pairs={{0,8},{8,16},{16,24},{24,32},{32,40},{40,48},{48,56},{56,64},{64,7... | collective-permute-start | bytes 49160 | tf_op jit(solution)/shard_map/ppermute | solution.py:16
  203.8 6.4 %collective-permute-start.30 = (f32[18,1,128]{2,1,0:T(1,128)S(1)}, f32[18,1,128]{2,1,0:T(1,128)S(1)}, u32[]{:S(2)}, u32[]{:S(2)}) collective-permute-start(f32[18,1,128]{2,1,0:T(1,128)S(1)} %get-tuple-element.67), channel_id=1, source_target_pairs={{1,0},{2,1},{3,2},{4,3},{5,4},{6,5},{7,6},{9,8},{10,9},{11,10},{12... | collective-permute-start | bytes 27656 | tf_op jit(solution)/shard_map/ppermute | solution.py:19
  205.1 5.9 %collective-permute-start.31 = (f32[18,1,128]{2,1,0:T(1,128)S(1)}, f32[18,1,128]{2,1,0:T(1,128)S(1)}, u32[]{:S(2)}, u32[]{:S(2)}) collective-permute-start(f32[18,1,128]{2,1,0:T(1,128)S(1)} %get-tuple-element.66), channel_id=1, source_target_pairs={{0,1},{1,2},{2,3},{3,4},{4,5},{5,6},{6,7},{8,9},{9,10},{10,11},{11... | collective-permute-start | bytes 27656 | tf_op jit(solution)/shard_map/ppermute | solution.py:16
  211.8 6.2 %collective-permute-start.32 = (f32[1,32,128]{2,1,0:T(8,128)S(1)}, f32[1,32,128]{2,1,0:T(8,128)S(1)}, u32[]{:S(2)}, u32[]{:S(2)}) collective-permute-start(f32[1,32,128]{2,1,0:T(8,128)S(1)} %get-tuple-element.75), channel_id=1, source_target_pairs={{8,0},{16,8},{24,16},{32,24},{40,32},{48,40},{56,48},{64,56},{72,6... | collective-permute-start | bytes 49160 | tf_op jit(solution)/shard_map/ppermute | solution.py:19
  213.7 5.6 %collective-permute-start.33 = (f32[1,32,128]{2,1,0:T(8,128)S(1)}, f32[1,32,128]{2,1,0:T(8,128)S(1)}, u32[]{:S(2)}, u32[]{:S(2)}) collective-permute-start(f32[1,32,128]{2,1,0:T(8,128)S(1)} %get-tuple-element.74), channel_id=1, source_target_pairs={{0,8},{8,16},{16,24},{24,32},{32,40},{40,48},{48,56},{56,64},{64,7... | collective-permute-start | bytes 49160 | tf_op jit(solution)/shard_map/ppermute | solution.py:16
  219.4 6.3 %collective-permute-start.34 = (f32[18,1,128]{2,1,0:T(1,128)S(1)}, f32[18,1,128]{2,1,0:T(1,128)S(1)}, u32[]{:S(2)}, u32[]{:S(2)}) collective-permute-start(f32[18,1,128]{2,1,0:T(1,128)S(1)} %get-tuple-element.65), channel_id=1, source_target_pairs={{1,0},{2,1},{3,2},{4,3},{5,4},{6,5},{7,6},{9,8},{10,9},{11,10},{12... | collective-permute-start | bytes 27656 | tf_op jit(solution)/shard_map/ppermute | solution.py:19
  220.7 5.6 %collective-permute-start.35 = (f32[18,1,128]{2,1,0:T(1,128)S(1)}, f32[18,1,128]{2,1,0:T(1,128)S(1)}, u32[]{:S(2)}, u32[]{:S(2)}) collective-permute-start(f32[18,1,128]{2,1,0:T(1,128)S(1)} %get-tuple-element.64), channel_id=1, source_target_pairs={{0,1},{1,2},{2,3},{3,4},{4,5},{5,6},{6,7},{8,9},{9,10},{10,11},{11... | collective-permute-start | bytes 27656 | tf_op jit(solution)/shard_map/ppermute | solution.py:16
  226.6 102.4 %copy-start.13 = (f32[6]{0:T(128)S(1)}, f32[6]{0:T(128)}, u32[]{:S(2)}) copy-start(f32[6]{0:T(128)} %constant.130) | copy-start | bytes 76
  227.8 103.5 %copy-start.6 = (f32[16,32,128]{2,1,0:T(8,128)}, f32[16,32,128]{2,1,0:T(8,128)S(1)}, u32[]{:S(2)}) copy-start(f32[16,32,128]{2,1,0:T(8,128)S(1)} %divide_add_fusion) | copy-start | bytes 786436
  228.7 100.9 %all-to-all-start = ((f32[32,32,128]{2,1,0:T(8,128)}), f32[32,32,128]{2,1,0:T(8,128)S(1)}, u32[]{:S(2)}, u32[]{:S(2)}) async-start(f32[32,32,128]{2,1,0:T(8,128)} %stack.3), calls=%async_computation | async-start | bytes 1048576 | tf_op jit(solution)/shard_map/all_to_all | solution.py:148
  (3 other events, 27.3 us)
